TPU v7x, 32 devices: a whole 2x2x4 slice. The times are simulated.
32 devices in a mesh: branch: 2 (over core), seq: 4 (over z), head: 4 (over y, x).
Axes of the slice: x: 2, y: 2, z: 4, core: 2. Of those that a mesh axis runs over, the one named last changes fastest.
Arguments:
- tokens: bfloat16 [1024, 3072], P('seq', 'head'), may hold values from -10 to 10
- valid_counts: int32 [4], P('seq'), may hold values from 1 to 256, 768 in all
- shared_qkv: bfloat16 [3072, 3, 1536], P('branch', None, 'head'), may hold values from -0.08479832 to 0.08479832
- shared_out: bfloat16 [1536, 3072], P('head', 'branch'), may hold values from -0.15625 to 0.15625
- skipped_qkv: bfloat16 [3072, 3, 1536], P('branch', None, 'head'), may hold values from -0.08479832 to 0.08479832
- skipped_out: bfloat16 [1536, 3072], P('head', 'branch'), may hold values from -0.15625 to 0.15625
- modulation: float32 [2, 3, 3072], replicated, may hold values from -3 to 3
- qk_gains: float32 [2, 2, 128], replicated, may hold values from 1.2 to 5.5
Outputs:
- branches: bfloat16 [2, 1024, 3072], P('branch', 'seq', 'head')
Inputs may be any that keep to these rules, and one draw needn't show every extreme that they name: `valid_counts`: each entry counts the leading real tokens of one shard of 256 slots; the rest are padding. The entries sum to 768 and one of them equals 256.
All inputs are finite; a program needn't handle non-finite values.
Results may differ from a plain program's by a relative error of at most 0.01.
Values may be sent and summed in bfloat16 or wider, within the bound.
No kernel may reach another device: no remote copies, remote signals or barrier semaphores. Data moves between devices by JAX's collectives and lax.ppermute only.
A program may use at most 128 MiB of HBM per device.

v0:
```python
import jax
import jax.numpy as jnp
from jax import lax
from jax.sharding import PartitionSpec as P

HEAD_DIM = 128


def modulate(x_rows, mod):
    whole = lax.all_gather(x_rows, "head", axis=1, tiled=True)
    xf = whole.astype(jnp.float32)
    mean = jnp.mean(xf, axis=1, keepdims=True)
    centered = xf - mean
    var = jnp.mean(centered * centered, axis=1, keepdims=True)
    normed = centered * lax.rsqrt(var + 1e-06)
    return (normed * (1.0 + mod[1]) + mod[0]).astype(jnp.bfloat16)


def attend_block(x_full, keep_full, qkv_weight, out_weight, mod, gains):
    rows, quarter = x_full.shape
    width = qkv_weight.shape[2]
    group = width // HEAD_DIM
    moded = modulate(x_full, mod)
    qkv = jnp.einsum(
        "rd,dsc->rsc",
        moded,
        lax.all_gather(qkv_weight, "branch", axis=0, tiled=True),
        preferred_element_type=jnp.float32,
    )
    qpart = qkv[:, 0].reshape(rows, group, HEAD_DIM)
    kpart = qkv[:, 1].reshape(rows, group, HEAD_DIM)
    query = (
        qpart * lax.rsqrt(jnp.mean(qpart * qpart, axis=2, keepdims=True) + 1e-06) * gains[0]
    ).astype(jnp.bfloat16)
    key = (
        kpart * lax.rsqrt(jnp.mean(kpart * kpart, axis=2, keepdims=True) + 1e-06) * gains[1]
    ).astype(jnp.bfloat16)
    key = key.reshape(rows, width)
    value = qkv[:, 2].astype(jnp.bfloat16)
    scale = 1.0 / HEAD_DIM**0.5
    keep_wire = keep_full.astype(jnp.bfloat16)
    peak = jnp.full((group, rows), -1e30, jnp.float32)
    key_piece = lax.all_gather(key, "seq", axis=0, tiled=True)
    value_piece = lax.all_gather(value, "seq", axis=0, tiled=True)
    keep_piece = lax.all_gather(keep_wire, "seq", axis=0, tiled=True)
    length = key_piece.shape[0]
    key_heads = key_piece.reshape(length, group, HEAD_DIM)
    value_heads = value_piece.reshape(length, group, HEAD_DIM)
    scores = (
        jnp.einsum("rhd,nhd->hrn", query, key_heads, preferred_element_type=jnp.float32) * scale
    )
    valid = keep_piece[None, None, :] > 0.5
    scores = jnp.where(valid, scores, -1e30)
    new_peak = jnp.maximum(peak, jnp.max(scores, axis=2))
    weights = jnp.where(valid, jnp.exp(scores - new_peak[:, :, None]), 0.0)
    total = jnp.sum(weights, axis=2)
    mixed = jnp.einsum(
        "hrn,nhd->hrd",
        weights.astype(jnp.bfloat16),
        value_heads,
        preferred_element_type=jnp.float32,
    )
    attended = (mixed / total[:, :, None]).astype(jnp.bfloat16)
    attended = attended.transpose(1, 0, 2).reshape(rows, width)
    projected = jnp.dot(
        attended,
        lax.all_gather(out_weight, "branch", axis=1, tiled=True),
        preferred_element_type=jnp.float32,
    )
    mine = lax.psum_scatter(projected, "head", scatter_dimension=1, tiled=True)
    gate = lax.dynamic_slice_in_dim(mod[2], lax.axis_index("head") * quarter, quarter, 0)
    return (x_full.astype(jnp.float32) + gate[None, :] * mine).astype(jnp.bfloat16)


def full_block(x_full, keep_full, qkv_weight, out_weight, mod, gains):
    updated = attend_block(x_full, keep_full, qkv_weight, out_weight, mod, gains)
    return updated


def per_device(
    tokens, valid_counts, shared_qkv, shared_out, skipped_qkv, skipped_out, modulation, qk_gains
):
    rows = tokens.shape[0]
    positions = jnp.arange(rows, dtype=jnp.int32)
    keep_all = (positions < valid_counts[0]).astype(jnp.float32)
    forked = full_block(tokens, keep_all, shared_qkv, shared_out, modulation[0], qk_gains[0])
    strong = full_block(forked, keep_all, skipped_qkv, skipped_out, modulation[1], qk_gains[1])
    result = jnp.where(lax.axis_index("branch") == 0, strong, forked)
    return result[None]


def solution(mesh):
    in_specs = (
        P("seq", "head"),
        P("seq"),
        P("branch", None, "head"),
        P("head", "branch"),
        P("branch", None, "head"),
        P("head", "branch"),
        P(),
        P(),
    )
    out_specs = P("branch", "seq", "head")
    return jax.shard_map(
        per_device, mesh=mesh, in_specs=in_specs, out_specs=out_specs, check_vma=False
    )
```

profile of v0, /device:TPU:0, one launch (start us, length us, event | category | flops | bytes accessed | tf_op | source)
XLA Modules:
  0.0 313.8 jit_solution(11347913517500845164)
XLA Ops:
  6.5 0.7 all-gather.10.cloned.1.call-update
  7.3 0.7 all-gather.12.cloned.1.call-update
  8.1 0.7 all-gather.14.cloned.1.call-update
  9.6 12.7 %all-gather.2 = bf16[4,1,256]{2,1,0:T(2,128)(2,1)S(1)} all-gather(bf16[1,1,256]{2,1,0:T(2,128)(2,1)S(1)} %reshape.146), channel_id=1, replica_groups=mesh['branch'=2,'seq'=4,'head'=4] {'seq'}, dimensions={0}, use_global_device_ids=true | all-gather | bytes 2560 | tf_op jit(solution)/shard_map/all_gather | solution.py:45
  22.3 20.5 %all-gather.10.cloned.1.call-done = bf16[256,3072]{1,0:T(8,128)(2,1)} async-done(((bf16[256,768]{1,0:T(8,128)(2,1)}), bf16[256,3072]{1,0:T(8,128)(2,1)}) %all-gather.10.cloned.1.call-update) | async-done | bytes 1572880 | tf_op jit(solution)/shard_map/all_gather | solution.py:10
  42.8 1.8 convert_reduce_fusion.1
  44.6 2.0 fusion.8
  46.6 15.7 %all-gather.12.cloned.1.call-done = bf16[3072,3,384]{2,0,1:T(8,128)(2,1)} async-done(((bf16[1536,3,384]{2,0,1:T(8,128)(2,1)}), bf16[3072,3,384]{2,0,1:T(8,128)(2,1)}) %all-gather.12.cloned.1.call-update) | async-done | bytes 7077904 | tf_op jit(solution)/shard_map/all_gather | solution.py:27
  62.3 5.3 %fusion.19 = f32[256,3,384]{2,0,1:T(8,128)S(1)} fusion(bf16[3072,3,384]{2,0,1:T(8,128)(2,1)} %all-gather.12.cloned.1.call-done, bf16[256,3072]{1,0:T(8,128)(2,1)S(1)} %copy-done, f32[3072]{0:T(1024)S(1)} %bitcast.90, f32[3072]{0:T(1024)S(1)} %bitcast.91, f32[256]{0:T(256)S(1)} %add_rsqrt_fusion.5, f32[256]{0:T(256)S(1)} %broadcast_multiply_fusion.1), kind=kOutput, calls=%fused_computation.27 | convolution fusion | flops 1816657920 | bytes 9857024 | tf_op jit(solution)/shard_map/rd,dsc->rsc/dot_general | solution.py:24
  68.1 19.8 %all_gather.37 = bf16[1024,384]{1,0:T(8,128)(2,1)S(1)} all-gather(bf16[256,384]{1,0:T(8,128)(2,1)S(1)} %fusion.61), channel_id=1, replica_groups=mesh['branch'=2,'seq'=4,'head'=4] {'seq'}, dimensions={0}, use_global_device_ids=true | all-gather | bytes 983040 | tf_op jit(solution)/shard_map/all_gather | solution.py:43
  88.4 18.0 %all-gather = bf16[1024,1,384]{2,0,1:T(8,128)(2,1)S(1)} all-gather(bf16[256,1,384]{2,0,1:T(8,128)(2,1)S(1)} %slice.109), channel_id=2, replica_groups=mesh['branch'=2,'seq'=4,'head'=4] {'seq'}, dimensions={0}, use_global_device_ids=true | all-gather | bytes 983040 | tf_op jit(solution)/shard_map/all_gather | solution.py:44
  106.8 0.8 fusion.12
  107.6 0.9 fusion.14
  108.5 0.9 fusion.53
  109.5 4.4 %fusion.78 = f32[256,3072]{1,0:T(8,128)} fusion(bf16[256,384]{0,1:T(8,128)(2,1)S(1)} %bitcast.87, bf16[384,3072]{1,0:T(8,128)(2,1)} %all-gather.14.cloned.1.call-done), kind=kOutput, calls=%fused_computation.104 | convolution fusion | flops 603979776 | bytes 5701632 | tf_op jit(solution)/shard_map/dot_general | solution.py:65
  114.0 43.3 %reduce-scatter.3.cloned.1.call-done = f32[256,768]{1,0:T(8,128)} async-done(((f32[256,3072]{1,0:T(8,128)}), f32[256,768]{1,0:T(8,128)}) %reduce-scatter.3.cloned.1.call-update) | async-done | bytes 786448 | tf_op jit(solution)/shard_map/reduce_scatter | solution.py:70
  157.3 2.0 add_convert_fusion.1
  159.4 0.5 all-gather.18.cloned.1.call-update
  159.9 0.7 all-gather.20.cloned.1.call-update
  160.7 29.6 %all-gather.16.cloned.1.call-done = bf16[256,3072]{1,0:T(8,128)(2,1)} async-done(((bf16[256,768]{1,0:T(8,128)(2,1)}), bf16[256,3072]{1,0:T(8,128)(2,1)}) %all-gather.16.cloned.1.call-update) | async-done | bytes 1572880 | tf_op jit(solution)/shard_map/all_gather | solution.py:10
  190.3 1.8 convert_reduce_fusion
  192.2 2.0 fusion.4
  194.1 15.5 %all-gather.18.cloned.1.call-done = bf16[3072,3,384]{2,0,1:T(8,128)(2,1)} async-done(((bf16[1536,3,384]{2,0,1:T(8,128)(2,1)}), bf16[3072,3,384]{2,0,1:T(8,128)(2,1)}) %all-gather.18.cloned.1.call-update) | async-done | bytes 7077904 | tf_op jit(solution)/shard_map/all_gather | solution.py:27
  209.7 5.3 %fusion.22 = f32[256,3,384]{2,0,1:T(8,128)S(1)} fusion(bf16[3072,3,384]{2,0,1:T(8,128)(2,1)} %all-gather.18.cloned.1.call-done, bf16[256,3072]{1,0:T(8,128)(2,1)S(1)} %copy-done.1, f32[3072]{0:T(1024)S(1)} %bitcast.88, f32[3072]{0:T(1024)S(1)} %bitcast.89, f32[256]{0:T(256)S(1)} %add_rsqrt_fusion.4, f32[256]{0:T(256)S(1)} %broadcast_multiply_fusion), kind=kOutput, calls=%fused_computation.29 | convolution fusion | flops 1816657920 | bytes 9857024 | tf_op jit(solution)/shard_map/rd,dsc->rsc/dot_general | solution.py:24
  215.5 19.8 %all_gather.42 = bf16[1024,384]{1,0:T(8,128)(2,1)S(1)} all-gather(bf16[256,384]{1,0:T(8,128)(2,1)S(1)} %fusion.59), channel_id=1, replica_groups=mesh['branch'=2,'seq'=4,'head'=4] {'seq'}, dimensions={0}, use_global_device_ids=true | all-gather | bytes 983040 | tf_op jit(solution)/shard_map/all_gather | solution.py:43
  235.8 18.2 %all-gather.1 = bf16[1024,1,384]{2,0,1:T(8,128)(2,1)S(1)} all-gather(bf16[256,1,384]{2,0,1:T(8,128)(2,1)S(1)} %slice.108), channel_id=3, replica_groups=mesh['branch'=2,'seq'=4,'head'=4] {'seq'}, dimensions={0}, use_global_device_ids=true | all-gather | bytes 983040 | tf_op jit(solution)/shard_map/all_gather | solution.py:44
  254.4 0.8 fusion.13
  255.2 0.9 fusion.16
  256.1 0.9 fusion.47
  257.1 4.4 %fusion.79 = f32[256,3072]{1,0:T(8,128)} fusion(bf16[256,384]{0,1:T(8,128)(2,1)S(1)} %bitcast.86, bf16[384,3072]{1,0:T(8,128)(2,1)} %all-gather.20.cloned.1.call-done), kind=kOutput, calls=%fused_computation.105 | convolution fusion | flops 603979776 | bytes 5701632 | tf_op jit(solution)/shard_map/dot_general | solution.py:65
  261.5 43.4 %reduce-scatter.5.cloned.1.call-done = f32[256,768]{1,0:T(8,128)} async-done(((f32[256,3072]{1,0:T(8,128)}), f32[256,768]{1,0:T(8,128)}) %reduce-scatter.5.cloned.1.call-update) | async-done | bytes 786448 | tf_op jit(solution)/shard_map/reduce_scatter | solution.py:70
  304.9 2.0 fusion.57
  (67 shorter events, 3.2 us)
Async XLA Ops:
  6.5 2.3 copy-start.4
  6.5 2.3 copy-start.5
  6.5 36.2 %all-gather.10.cloned.1.call-start = ((), (), s32[]{:S(2)}) async-start(), calls=%async_computation.2 | async-start | bytes 1966080 | tf_op jit(solution)/shard_map/all_gather | solution.py:10
  7.3 55.0 %all-gather.12.cloned.1.call-start = ((), (), s32[]{:S(2)}) async-start(), calls=%async_computation.3 | async-start | bytes 10616832 | tf_op jit(solution)/shard_map/all_gather | solution.py:27
  8.0 101.5 %all-gather.14.cloned.1.call-start = ((), (), s32[]{:S(2)}) async-start(), calls=%async_computation.4 | async-start | bytes 3538944 | tf_op jit(solution)/shard_map/all_gather | solution.py:67
  8.7 148.6 %reduce-scatter.3.cloned.1.call-start = ((), (), s32[]{:S(2)}) async-start(), calls=%async_computation.5 | async-start | bytes 3932160 | tf_op jit(solution)/shard_map/reduce_scatter | solution.py:70
  42.8 19.5 %copy-start = (bf16[256,3072]{1,0:T(8,128)(2,1)S(1)}, bf16[256,3072]{1,0:T(8,128)(2,1)}, u32[]{:S(2)}) copy-start(bf16[256,3072]{1,0:T(8,128)(2,1)} %all-gather.10.cloned.1.call-done) | copy-start | bytes 4718596
  109.5 47.8 %copy-start.3 = (bf16[256,768]{1,0:T(8,128)(2,1)S(1)}, bf16[256,768]{1,0:T(8,128)(2,1)}, u32[]{:S(2)}) copy-start(bf16[256,768]{1,0:T(8,128)(2,1)} %param.8) | copy-start | bytes 1179652
  113.9 76.4 %all-gather.16.cloned.1.call-start = ((), (), s32[]{:S(2)}) async-start(), calls=%async_computation.6 | async-start | bytes 1966080 | tf_op jit(solution)/shard_map/all_gather | solution.py:10
  159.3 50.4 %all-gather.18.cloned.1.call-start = ((), (), s32[]{:S(2)}) async-start(), calls=%async_computation.7 | async-start | bytes 10616832 | tf_op jit(solution)/shard_map/all_gather | solution.py:27
  159.9 97.1 %all-gather.20.cloned.1.call-start = ((), (), s32[]{:S(2)}) async-start(), calls=%async_computation.8 | async-start | bytes 3538944 | tf_op jit(solution)/shard_map/all_gather | solution.py:67
  160.6 144.3 %reduce-scatter.5.cloned.1.call-start = ((), (), s32[]{:S(2)}) async-start(), calls=%async_computation.9 | async-start | bytes 3932160 | tf_op jit(solution)/shard_map/reduce_scatter | solution.py:70
  190.3 19.3 %copy-start.1 = (bf16[256,3072]{1,0:T(8,128)(2,1)S(1)}, bf16[256,3072]{1,0:T(8,128)(2,1)}, u32[]{:S(2)}) copy-start(bf16[256,3072]{1,0:T(8,128)(2,1)} %all-gather.16.cloned.1.call-done) | copy-start | bytes 4718596
  257.0 47.9 %copy-start.2 = (bf16[256,768]{1,0:T(8,128)(2,1)S(1)}, bf16[256,768]{1,0:T(8,128)(2,1)}, u32[]{:S(2)}) copy-start(bf16[256,768]{1,0:T(8,128)(2,1)} %add_convert_fusion.1) | copy-start | bytes 1179652
Sparse Core Ops, SparseCore 0:
  9.2 33.5 all-gather.9
  44.3 17.9 all-gather.11
  63.8 12.1 all-gather.13
  114.0 43.2 reduce-scatter.2
  159.4 30.8 all-gather.15
  191.7 17.9 all-gather.17
  211.2 12.1 all-gather.19
  261.6 43.2 reduce-scatter.4
where the time goes:
time: 314 us
  waiting for transfers between devices  172 us (55%)
  blocking collectives  88.5 us (28%)
  matrix products  22.8 us (7%)
  between operations  14.5 us (5%)
  other arithmetic  13.9 us (4%)
    reduce_scatter x2, waiting for transfers between devices, attend_block(): mine = lax.psum_scatter(projected, 'head', scatter_dimension=1, tiled=True)  86.7 us
    all_gather x2, waiting for transfers between devices, modulate(): whole = lax.all_gather(x_rows, 'head', axis=1, tiled=True)  50.1 us
    all_gather x2, blocking collectives, attend_block(): key_piece = lax.all_gather(key, 'seq', axis=0, tiled=True)  39.7 us
    all_gather x2, blocking collectives, attend_block(): value_piece = lax.all_gather(value, 'seq', axis=0, tiled=True)  36.2 us
    all_gather x2, waiting for transfers between devices, attend_block(): lax.all_gather(qkv_weight, 'branch', axis=0, tiled=True)  31.2 us
    all_gather x1, blocking collectives, attend_block(): keep_piece = lax.all_gather(keep_wire, 'seq', axis=0, tiled=True)  12.7 us
    dot_general x2, matrix products, attend_block(): jnp.einsum('rd,dsc->rsc', moded, lax.all_gather(qkv_weight, 'branch', axi...  10.5 us
    dot_general x2, matrix products, attend_block(): jnp.dot(attended, lax.all_gather(out_weight, 'branch', axis=1, tiled=True...  8.77 us
  transfers between devices with their start and end apart: 8, of which 6 were waited for; matrix products, arithmetic and copies ran while one was open for 8% of the time, Pallas kernels for 0%

commit v1 on v0

--- a/solution.py
+++ b/solution.py
@@ -6,8 +6,29 @@
 HEAD_DIM = 128
 
 
+def in_order(pieces, dim):
+    shape = list(pieces.shape[1:])
+    shape[dim] *= pieces.shape[0]
+    return jnp.moveaxis(pieces, 0, dim).reshape(shape)
+
+
+def collected_by_bits(x, axis):
+    devices, index = (lax.axis_size(axis), lax.axis_index(axis))
+    pieces, bit = (x[None], 1)
+    while bit < devices:
+        other = lax.ppermute(pieces, axis, [(i, i ^ bit) for i in range(devices)])
+        low = index & bit == 0
+        pieces = jnp.concatenate([jnp.where(low, pieces, other), jnp.where(low, other, pieces)])
+        bit *= 2
+    return pieces
+
+
+def collect(shard, axis, dim):
+    return in_order(collected_by_bits(shard, axis), dim)
+
+
 def modulate(x_rows, mod):
-    whole = lax.all_gather(x_rows, "head", axis=1, tiled=True)
+    whole = collect(x_rows, "head", 1)
     xf = whole.astype(jnp.float32)
     mean = jnp.mean(xf, axis=1, keepdims=True)
     centered = xf - mean

time: 314 us -> 278 us (0.89)
  waiting for transfers between devices: 172 us -> 125 us
  starting transfers between devices: 0.28 us -> 7.99 us
  local copies, waits for them, and re-layouts: 2.33 us -> 9.4 us
  blocking collectives: 88.5 us -> 82.3 us
    all_gather x2 -> x0, waiting for transfers between devices: 50.1 us -> none  [modulate(): whole = lax.all_gather(x_rows, 'head', axis=1, tiled=True)]
    ppermute x0 -> x4, waiting for transfers between devices: none -> 39.9 us  [collected_by_bits(): other = lax.ppermute(pieces, axis, [(i, i ^ bit) for i in range(devices)])]
    all_gather x2, waiting for transfers between devices: 31.2 us -> 0.04 us  [attend_block(): lax.all_gather(qkv_weight, 'branch', axis=0, tiled=True)]
    ppermute x0 -> x4, starting transfers between devices: none -> 7.61 us  [collected_by_bits(): other = lax.ppermute(pieces, axis, [(i, i ^ bit) for i in range(devices)])]
    convert_element_type x0 -> x4, other arithmetic: none -> 7.3 us  [the longest x2 6.89 us: modulate(): return (normed * (1.0 + mod[1]) + mod[0]).astype(jnp.bfloat16)]
    convert_element_type x0 -> x2, local copies, waits for them, and re-layouts: none -> 4.8 us  [modulate(): xf = whole.astype(jnp.float32)]
    all_gather x2, blocking collectives: 39.7 us -> 36.3 us  [attend_block(): key_piece = lax.all_gather(key, 'seq', axis=0, tiled=True)]
    reduce_scatter x2, waiting for transfers between devices: 86.7 us -> 83.5 us  [attend_block(): mine = lax.psum_scatter(projected, 'head', scatter_dimension=1, tiled=True)]
  transfers between devices with their start and end apart: 8 -> 10, of which waited for: 6 -> 5; matrix products, arithmetic and copies ran while one was open for 8% -> 13% of each run, Pallas kernels for 0% -> 0%
where the time goes in v1:
time: 278 us
  waiting for transfers between devices  125 us (45%)
  blocking collectives  82.3 us (30%)
  matrix products  22.7 us (8%)
  other arithmetic  16.2 us (6%)
  between operations  14.5 us (5%)
  local copies, waits for them, and re-layouts  9.4 us (3%)
  starting transfers between devices  7.99 us (3%)
    reduce_scatter x2, waiting for transfers between devices, attend_block(): mine = lax.psum_scatter(projected, 'head', scatter_dimension=1, tiled=True)  83.5 us
    ppermute x4, waiting for transfers between devices, collected_by_bits(): other = lax.ppermute(pieces, axis, [(i, i ^ bit) for i in range(devices)])  39.9 us
    all_gather x2, blocking collectives, attend_block(): key_piece = lax.all_gather(key, 'seq', axis=0, tiled=True)  36.3 us
    all_gather x2, blocking collectives, attend_block(): value_piece = lax.all_gather(value, 'seq', axis=0, tiled=True)  34.8 us
    all_gather x1, blocking collectives, attend_block(): keep_piece = lax.all_gather(keep_wire, 'seq', axis=0, tiled=True)  11.2 us
    dot_general x2, matrix products, attend_block(): jnp.einsum('rd,dsc->rsc', moded, lax.all_gather(qkv_weight, 'branch', axi...  10.5 us
    dot_general x2, matrix products, attend_block(): jnp.dot(attended, lax.all_gather(out_weight, 'branch', axis=1, tiled=True...  8.71 us
    ppermute x4, starting transfers between devices, collected_by_bits(): other = lax.ppermute(pieces, axis, [(i, i ^ bit) for i in range(devices)])  7.61 us
  transfers between devices with their start and end apart: 10, of which 5 were waited for; matrix products, arithmetic and copies ran while one was open for 13% of the time, Pallas kernels for 0%

profile of v1, /device:TPU:0, one launch (start us, length us, event | category | flops | bytes accessed | tf_op | source)
XLA Modules:
  0.0 277.8 jit_solution(3893638836795919860)
XLA Ops:
  6.5 0.7 all-gather.8.cloned.1.call-update
  7.5 3.0 %collective-permute-start = (bf16[1,256,768]{2,1,0:T(8,128)(2,1)S(1)}, bf16[1,256,768]{2,1,0:T(8,128)(2,1)S(1)}, u32[]{:S(2)}, u32[]{:S(2)}) collective-permute-start(bf16[1,256,768]{2,1,0:T(8,128)(2,1)S(1)} %bitcast.115), channel_id=1, source_target_pairs={{0,1},{1,0},{2,3},{3,2},{4,5},{5,4},{6,7},{7,6},{8,9},{9,8},{10,11... | collective-permute-start | bytes 1179656 | tf_op jit(solution)/shard_map/ppermute | solution.py:19
  11.2 11.2 %all-gather.2 = bf16[4,1,256]{2,1,0:T(2,128)(2,1)S(1)} all-gather(bf16[1,1,256]{2,1,0:T(2,128)(2,1)S(1)} %reshape.164), channel_id=1, replica_groups=mesh['branch'=2,'seq'=4,'head'=4] {'seq'}, dimensions={0}, use_global_device_ids=true | all-gather | bytes 2560 | tf_op jit(solution)/shard_map/all_gather | solution.py:66
  23.2 1.6 collective-permute-start.1
  25.5 14.8 %collective-permute-done.1 = bf16[2,256,768]{2,1,0:T(8,128)(2,1)S(1)} collective-permute-done((bf16[2,256,768]{2,1,0:T(8,128)(2,1)S(1)}, bf16[2,256,768]{2,1,0:T(8,128)(2,1)S(1)}, u32[]{:S(2)}, u32[]{:S(2)}) %collective-permute-start.1) | collective-permute-done | bytes 786464 | tf_op jit(solution)/shard_map/ppermute | solution.py:19
  41.4 2.4 copy.35
  43.8 3.1 %fusion.11 = bf16[256,3072]{0,1:T(8,128)(2,1)S(1)} fusion(f32[256,4,768]{0,2,1:T(8,128)} %copy.35, f32[3072]{0:T(1024)S(1)} %bitcast.122, f32[3072]{0:T(1024)S(1)} %bitcast.123, f32[256]{0:T(256)S(1)} %add_rsqrt_fusion.5, f32[256]{0:T(256)S(1)} %broadcast_multiply_fusion.1), kind=kLoop, calls=%fused_computation.19 | loop fusion | flops 3932160 | bytes 4745216 | tf_op jit(solution)/shard_map/convert_element_type | solution.py:37
  46.9 5.2 %fusion.20 = f32[256,3,384]{2,0,1:T(8,128)S(1)} fusion(bf16[3072,3,384]{2,0,1:T(8,128)(2,1)} %all-gather.8.cloned.1.call-done, bf16[256,3072]{0,1:T(8,128)(2,1)S(1)} %fusion.11), kind=kOutput, calls=%fused_computation.34 | convolution fusion | flops 1811939328 | bytes 9830400 | tf_op jit(solution)/shard_map/rd,dsc->rsc/dot_general | solution.py:45
  52.8 17.8 %all_gather.30 = bf16[1024,384]{1,0:T(8,128)(2,1)S(1)} all-gather(bf16[256,384]{1,0:T(8,128)(2,1)S(1)} %fusion.51), channel_id=1, replica_groups=mesh['branch'=2,'seq'=4,'head'=4] {'seq'}, dimensions={0}, use_global_device_ids=true | all-gather | bytes 983040 | tf_op jit(solution)/shard_map/all_gather | solution.py:64
  71.0 17.4 %all-gather = bf16[1024,1,384]{2,0,1:T(8,128)(2,1)S(1)} all-gather(bf16[256,1,384]{2,0,1:T(8,128)(2,1)S(1)} %slice.109), channel_id=2, replica_groups=mesh['branch'=2,'seq'=4,'head'=4] {'seq'}, dimensions={0}, use_global_device_ids=true | all-gather | bytes 983040 | tf_op jit(solution)/shard_map/all_gather | solution.py:65
  88.8 0.8 fusion.12
  89.6 0.9 fusion.14
  90.5 0.9 fusion.43
  91.5 4.4 %fusion.68 = f32[256,3072]{1,0:T(8,128)} fusion(bf16[256,384]{0,1:T(8,128)(2,1)S(1)} %bitcast.119, bf16[384,3072]{1,0:T(8,128)(2,1)} %all-gather.10.cloned.1.call-done), kind=kOutput, calls=%fused_computation.112 | convolution fusion | flops 603979776 | bytes 5701632 | tf_op jit(solution)/shard_map/dot_general | solution.py:86
  96.5 42.1 %reduce-scatter.3.cloned.1.call-done = f32[256,768]{1,0:T(8,128)} async-done(((f32[256,3072]{1,0:T(8,128)}), f32[256,768]{1,0:T(8,128)}) %reduce-scatter.3.cloned.1.call-update) | async-done | bytes 786448 | tf_op jit(solution)/shard_map/reduce_scatter | solution.py:91
  138.7 1.2 add_convert_fusion.1
  139.9 1.5 collective-permute-start.2
  141.4 9.2 %collective-permute-done.2 = bf16[1,256,768]{2,1,0:T(8,128)(2,1)S(1)} collective-permute-done((bf16[1,256,768]{2,1,0:T(8,128)(2,1)S(1)}, bf16[1,256,768]{2,1,0:T(8,128)(2,1)S(1)}, u32[]{:S(2)}, u32[]{:S(2)}) %collective-permute-start.2) | collective-permute-done | bytes 393248 | tf_op jit(solution)/shard_map/ppermute | solution.py:19
  150.8 1.5 collective-permute-start.3
  153.2 15.9 %collective-permute-done.3 = bf16[2,256,768]{2,1,0:T(8,128)(2,1)S(1)} collective-permute-done((bf16[2,256,768]{2,1,0:T(8,128)(2,1)S(1)}, bf16[2,256,768]{2,1,0:T(8,128)(2,1)S(1)}, u32[]{:S(2)}, u32[]{:S(2)}) %collective-permute-start.3) | collective-permute-done | bytes 786464 | tf_op jit(solution)/shard_map/ppermute | solution.py:19
  170.9 2.4 copy.44
  173.3 3.8 %fusion.7 = bf16[256,3072]{0,1:T(8,128)(2,1)S(1)} fusion(f32[256,4,768]{0,2,1:T(8,128)} %copy.44, f32[3072]{0:T(1024)S(1)} %bitcast.120, f32[3072]{0:T(1024)} %bitcast.121, f32[256]{0:T(256)} %add_rsqrt_fusion.4, f32[256]{0:T(256)} %copy-done.3), kind=kLoop, calls=%fused_computation.14 | loop fusion | flops 3932160 | bytes 4745216 | tf_op jit(solution)/shard_map/convert_element_type | solution.py:37
  177.2 5.2 %fusion.18 = f32[256,3,384]{2,0,1:T(8,128)S(1)} fusion(bf16[3072,3,384]{2,0,1:T(8,128)(2,1)} %all-gather.12.cloned.1.call-done, bf16[256,3072]{0,1:T(8,128)(2,1)S(1)} %fusion.7), kind=kOutput, calls=%fused_computation.32 | convolution fusion | flops 1811939328 | bytes 9830400 | tf_op jit(solution)/shard_map/rd,dsc->rsc/dot_general | solution.py:45
  183.2 18.5 %all_gather.34 = bf16[1024,384]{1,0:T(8,128)(2,1)S(1)} all-gather(bf16[256,384]{1,0:T(8,128)(2,1)S(1)} %fusion.49), channel_id=1, replica_groups=mesh['branch'=2,'seq'=4,'head'=4] {'seq'}, dimensions={0}, use_global_device_ids=true | all-gather | bytes 983040 | tf_op jit(solution)/shard_map/all_gather | solution.py:64
  202.1 17.4 %all-gather.1 = bf16[1024,1,384]{2,0,1:T(8,128)(2,1)S(1)} all-gather(bf16[256,1,384]{2,0,1:T(8,128)(2,1)S(1)} %slice.108), channel_id=3, replica_groups=mesh['branch'=2,'seq'=4,'head'=4] {'seq'}, dimensions={0}, use_global_device_ids=true | all-gather | bytes 983040 | tf_op jit(solution)/shard_map/all_gather | solution.py:65
  219.9 0.8 fusion.13
  220.7 0.9 fusion.16
  221.6 0.9 fusion.37
  222.6 4.3 %fusion.69 = f32[256,3072]{1,0:T(8,128)} fusion(bf16[256,384]{0,1:T(8,128)(2,1)S(1)} %bitcast.118, bf16[384,3072]{1,0:T(8,128)(2,1)} %all-gather.14.cloned.1.call-done), kind=kOutput, calls=%fused_computation.113 | convolution fusion | flops 603979776 | bytes 5701632 | tf_op jit(solution)/shard_map/dot_general | solution.py:86
  227.0 0.7 dynamic-slice_reduce_fusion
  227.7 41.3 %reduce-scatter.5.cloned.1.call-done = f32[256,768]{1,0:T(8,128)} async-done(((f32[256,3072]{1,0:T(8,128)}), f32[256,768]{1,0:T(8,128)}) %reduce-scatter.5.cloned.1.call-update) | async-done | bytes 786448 | tf_op jit(solution)/shard_map/reduce_scatter | solution.py:91
  269.0 2.0 fusion.47
  (85 shorter events, 9.3 us)
Async XLA Ops:
  6.5 1.0 copy-start
  6.5 15.9 %copy-start.6 = (f32[2,2,128]{2,1,0:T(2,128)S(1)}, f32[2,2,128]{2,1,0:T(2,128)}, u32[]{:S(2)}) copy-start(f32[2,2,128]{2,1,0:T(2,128)} %param.15) | copy-start | bytes 6148
  6.5 40.4 %all-gather.8.cloned.1.call-start = ((), (), s32[]{:S(2)}) async-start(), calls=%async_computation.2 | async-start | bytes 10616832 | tf_op jit(solution)/shard_map/all_gather | solution.py:48
  6.5 18.2 %copy-start.2 = (f32[2,3,3072]{2,0,1:T(2,128)S(1)}, f32[2,3,3072]{2,0,1:T(2,128)}, u32[]{:S(2)}) copy-start(f32[2,3,3072]{2,0,1:T(2,128)} %param.14) | copy-start | bytes 221188
  7.3 84.2 %all-gather.10.cloned.1.call-start = ((), (), s32[]{:S(2)}) async-start(), calls=%async_computation.3 | async-start | bytes 3538944 | tf_op jit(solution)/shard_map/all_gather | solution.py:88
  7.5 15.5 %collective-permute-start = (bf16[1,256,768]{2,1,0:T(8,128)(2,1)S(1)}, bf16[1,256,768]{2,1,0:T(8,128)(2,1)S(1)}, u32[]{:S(2)}, u32[]{:S(2)}) collective-permute-start(bf16[1,256,768]{2,1,0:T(8,128)(2,1)S(1)} %bitcast.115), channel_id=1, source_target_pairs={{0,1},{1,0},{2,3},{3,2},{4,5},{5,4},{6,7},{7,6},{8,9},{9,8},{10,11... | collective-permute-start | bytes 1179656 | tf_op jit(solution)/shard_map/ppermute | solution.py:19
  10.5 128.2 %reduce-scatter.3.cloned.1.call-start = ((), (), s32[]{:S(2)}) async-start(), calls=%async_computation.4 | async-start | bytes 3932160 | tf_op jit(solution)/shard_map/reduce_scatter | solution.py:91
  23.2 17.0 %collective-permute-start.1 = (bf16[2,256,768]{2,1,0:T(8,128)(2,1)S(1)}, bf16[2,256,768]{2,1,0:T(8,128)(2,1)S(1)}, u32[]{:S(2)}, u32[]{:S(2)}) collective-permute-start(bf16[2,256,768]{2,1,0:T(8,128)(2,1)S(1)} %pad_maximum_fusion.2), channel_id=1, source_target_pairs={{0,2},{1,3},{2,0},{3,1},{4,6},{5,7},{6,4},{7,5},{8,10},{9,11},{10,... | collective-permute-start | bytes 2359304 | tf_op jit(solution)/shard_map/ppermute | solution.py:19
  95.9 42.8 %copy-start.1 = (bf16[256,768]{1,0:T(8,128)(2,1)S(1)}, bf16[256,768]{1,0:T(8,128)(2,1)}, u32[]{:S(2)}) copy-start(bf16[256,768]{1,0:T(8,128)(2,1)} %param.8) | copy-start | bytes 1179652
  95.9 81.3 %all-gather.12.cloned.1.call-start = ((), (), s32[]{:S(2)}) async-start(), calls=%async_computation.5 | async-start | bytes 10616832 | tf_op jit(solution)/shard_map/all_gather | solution.py:48
  96.5 56.1 %copy-start.7 = (f32[128]{0:T(128)S(1)}, f32[128]{0:T(128)}, u32[]{:S(2)}) copy-start(f32[128]{0:T(128)} %get-tuple-element.26) | copy-start | bytes 1540
  96.5 126.1 %all-gather.14.cloned.1.call-start = ((), (), s32[]{:S(2)}) async-start(), calls=%async_computation.6 | async-start | bytes 3538944 | tf_op jit(solution)/shard_map/all_gather | solution.py:88
  139.9 10.7 %collective-permute-start.2 = (bf16[1,256,768]{2,1,0:T(8,128)(2,1)S(1)}, bf16[1,256,768]{2,1,0:T(8,128)(2,1)S(1)}, u32[]{:S(2)}, u32[]{:S(2)}) collective-permute-start(bf16[1,256,768]{2,1,0:T(8,128)(2,1)S(1)} %bitcast.108), channel_id=1, source_target_pairs={{0,1},{1,0},{2,3},{3,2},{4,5},{5,4},{6,7},{7,6},{8,9},{9,8},{10,11... | collective-permute-start | bytes 1179656 | tf_op jit(solution)/shard_map/ppermute | solution.py:19
  150.8 18.3 %collective-permute-start.3 = (bf16[2,256,768]{2,1,0:T(8,128)(2,1)S(1)}, bf16[2,256,768]{2,1,0:T(8,128)(2,1)S(1)}, u32[]{:S(2)}, u32[]{:S(2)}) collective-permute-start(bf16[2,256,768]{2,1,0:T(8,128)(2,1)S(1)} %pad_maximum_fusion.3), channel_id=1, source_target_pairs={{0,2},{1,3},{2,0},{3,1},{4,6},{5,7},{6,4},{7,5},{8,10},{9,11},{10,... | collective-permute-start | bytes 2359304 | tf_op jit(solution)/shard_map/ppermute | solution.py:19
  152.3 116.7 %reduce-scatter.5.cloned.1.call-start = ((), (), s32[]{:S(2)}) async-start(), calls=%async_computation.7 | async-start | bytes 3932160 | tf_op jit(solution)/shard_map/reduce_scatter | solution.py:91
  169.7 0.6 copy-start.3
  182.4 0.7 copy-start.4
  183.2 36.7 %copy-start.5 = (f32[128]{0:T(128)S(1)}, f32[128]{0:T(128)}, u32[]{:S(2)}) copy-start(f32[128]{0:T(128)} %get-tuple-element.23) | copy-start | bytes 1540
Sparse Core Ops, SparseCore 0:
  8.9 20.6 all-gather.7
  31.1 12.1 all-gather.9
  96.0 42.6 reduce-scatter.2
  140.1 17.8 all-gather.11
  159.4 12.1 all-gather.13
  227.1 41.8 reduce-scatter.4
